TPU v7x, 512 devices: a whole 4x4x16 slice. The times are simulated.
512 devices in a mesh: grid: 64 (over y, z), state: 8 (over x, core).
Axes of the slice: x: 4, y: 4, z: 16, core: 2. Of those that a mesh axis runs over, the one named last changes fastest.
Arguments:
- orbitals: float32 [8, 512, 64, 128], P('state', 'grid'), may hold values from -6 to 6
- potential: float32 [512, 64, 128], P('grid'), may hold values from 0 to 2
Outputs:
- corrections: float32 [8, 512, 64, 128], P('state', 'grid')
- correlation_gram: float32 [8, 8], P('state')
All inputs are finite; a program needn't handle non-finite values.
Results may differ from a plain program's by a relative error of at most 0.00095.
Values may be sent and summed in bfloat16 or wider, within the bound.
A program may use at most 64 MiB of HBM per device.

v0:
```python
import jax
import jax.numpy as jnp
from jax import lax
from jax.sharding import PartitionSpec as P

LEVELS = 4
COARSE_SWEEPS = 3
CENTER = -2.5
NEAR_COEF = 4.0 / 3.0
FAR_COEF = -1.0 / 12.0
SHIFT_TERM = 0.25
DAMPING = 2.0 / 3.0


def with_halo(block, sides, width):
    for axis, dim in sides:
        count = lax.axis_size(axis)
        forward = [(i, i + 1) for i in range(count - 1)]
        forward.append((count - 1, 0))
        backward = [(target, source) for source, target in forward]
        low = lax.ppermute(
            lax.slice_in_dim(block, block.shape[dim] - width, None, axis=dim), axis, forward
        )
        high = lax.ppermute(lax.slice_in_dim(block, 0, width, axis=dim), axis, backward)
        block = jnp.concatenate([low, block, high], axis=dim)
    return block


def laplace_four(values, axis):
    near = jnp.roll(values, 1, axis) + jnp.roll(values, -1, axis)
    far = jnp.roll(values, 2, axis) + jnp.roll(values, -2, axis)
    return CENTER * values + NEAR_COEF * near + FAR_COEF * far


def face_halo(values):
    return with_halo(values.astype(jnp.bfloat16), (("grid", 1),), 1).astype(values.dtype)


def level_apply(values, padded, inverse):
    beside = padded[:, 2:] + padded[:, :-2]
    beside = beside + jnp.roll(values, 1, 2) + jnp.roll(values, -1, 2)
    beside = beside + jnp.roll(values, 1, 3) + jnp.roll(values, -1, 3)
    return (SHIFT_TERM + 3.0 * inverse) * values - 0.5 * inverse * beside


def restrict(values):
    count, sx, sy, sz = values.shape
    shaped = values.reshape(count, sx // 2, 2, sy // 2, 2, sz // 2, 2)
    return jnp.mean(shaped, axis=(2, 4, 6))


def prolong(values):
    return jnp.repeat(jnp.repeat(jnp.repeat(values, 2, 1), 2, 2), 2, 3)


def jacobi_sweep(iterate, source, inverse, padder):
    diagonal = SHIFT_TERM + 3.0 * inverse
    applied = level_apply(iterate, padder(iterate), inverse)
    return iterate + DAMPING * (source - applied) / diagonal


def coarse_solve(source, inverse, padder):
    diagonal = SHIFT_TERM + 3.0 * inverse
    iterate = DAMPING * source / diagonal
    for repeat in range(COARSE_SWEEPS - 1):
        iterate = jacobi_sweep(iterate, source, inverse, padder)
    return iterate


def vcycle(source, depth_level):
    inverse = 0.25**depth_level
    diagonal = SHIFT_TERM + 3.0 * inverse
    if depth_level == LEVELS - 1:
        return coarse_solve(source, inverse, face_halo)
    iterate = DAMPING * source / diagonal
    remainder = source - level_apply(iterate, face_halo(iterate), inverse)
    coarse_error = vcycle(restrict(remainder), depth_level + 1)
    iterate = iterate + prolong(coarse_error)
    return jacobi_sweep(iterate, source, inverse, face_halo)


def on_device(orbitals, potential):
    padded = with_halo(orbitals, (("grid", 1),), 2)
    near = padded[:, 3:-1] + padded[:, 1:-3]
    far = padded[:, 4:] + padded[:, :-4]
    lap_first = CENTER * orbitals + NEAR_COEF * near + FAR_COEF * far
    lap = lap_first + laplace_four(orbitals, 2) + laplace_four(orbitals, 3)
    hpsi = -0.5 * lap + potential[None] * orbitals
    numer, denom = lax.psum(
        (jnp.sum(orbitals * hpsi, axis=(1, 2, 3)), jnp.sum(orbitals * orbitals, axis=(1, 2, 3))),
        "grid",
    )
    energy = numer / denom
    residual = hpsi - energy[:, None, None, None] * orbitals
    corrections = vcycle(residual, 0)
    count = corrections.shape[0]
    rounded = corrections.astype(jnp.bfloat16).reshape(count, -1)
    row_block = jnp.einsum(
        "ac,bc->ab",
        rounded,
        lax.all_gather(rounded, "state", axis=0, tiled=True),
        preferred_element_type=jnp.float32,
    )
    summed = lax.psum(row_block, "grid")
    correlation_gram = summed / jnp.float32(rounded.shape[1] * lax.axis_size("grid"))
    return (corrections, correlation_gram)


def solution(mesh):
    placed = (P("state", "grid", None, None), P("grid", None, None))
    return jax.shard_map(
        on_device,
        mesh=mesh,
        in_specs=placed,
        out_specs=(P("state", "grid", None, None), P("state", None)),
        check_vma=False,
    )
```

profile of v0, /device:TPU:4, one launch (start us, length us, event | category | flops | bytes accessed | tf_op | source)
XLA Modules:
  0.0 495.5 jit_solution(615986933523737960)
XLA Ops:
  7.2 1.5 fusion.122
  8.7 3.8 collective-permute-start.1
  12.5 11.9 %collective-permute-start = (f32[1,2,64,128]{3,2,1,0:T(8,128)}, f32[1,2,64,128]{3,2,1,0:T(8,128)S(1)}, u32[]{:S(2)}, u32[]{:S(2)}) collective-permute-start(f32[1,2,64,128]{3,2,1,0:T(8,128)} %get-tuple-element.64), channel_id=1, source_target_pairs={{8,0},{16,8},{24,16},{32,24},{40,32},{48,40},{56,48},{64,56},{72,6... | collective-permute-start | bytes 196616 | tf_op jit(solution)/shard_map/ppermute | solution.py:24
  24.5 0.8 fusion.123
  25.3 0.8 fusion.124
  26.1 1.2 copy.115
  27.3 1.0 fusion.117
  28.3 1.0 fusion.115
  29.3 1.2 fusion.113
  30.5 1.1 fusion.112
  31.7 0.6 fusion.114
  32.3 0.3 copy.125
  32.5 0.3 copy.121
  32.8 0.3 copy.127
  33.1 0.3 copy.123
  33.3 1.0 copy.136
  34.3 0.7 multiply_reduce_fusion.1
  35.1 1.0 copy.154
  36.1 0.8 fusion.119
  36.9 2.0 copy.153
  38.9 1.0 copy.155
  39.9 1.0 copy.156
  40.9 4.4 multiply_reduce_fusion
  45.3 140.7 %all-reduce = (f32[1]{0:T(128)}, f32[1]{0:T(128)}) all-reduce(f32[1]{0:T(128)} %bitcast.1, f32[1]{0:T(128)} %bitcast.2), channel_id=1, replica_groups=mesh['grid'=64,'state'=8] {'grid'}, use_global_device_ids=true, to_apply=%region_1.2 | all-reduce | flops 2 | bytes 16 | tf_op jit(solution)/shard_map/psum | solution.py:89
  187.7 0.2 fusion.111
  188.0 1.9 collective-permute-start.2
  190.0 7.2 %collective-permute-start.3 = (bf16[1,1,64,128]{2,1,3,0:T(2,128)(2,1)S(1)}, bf16[1,1,64,128]{2,1,3,0:T(2,128)(2,1)S(1)}, u32[]{:S(2)}, u32[]{:S(2)}) collective-permute-start(bf16[1,1,64,128]{2,1,3,0:T(2,128)(2,1)S(1)} %get-tuple-element.59), channel_id=1, source_target_pairs={{8,0},{16,8},{24,16},{32,24},{40,32},{48,40},{56,48},{64,56},{72,6... | collective-permute-start | bytes 49160 | tf_op jit(solution)/shard_map/ppermute | solution.py:24
  197.2 0.3 collective-permute-done.2
  197.5 1.6 collective-permute-done.3
  199.1 0.3 maximum_convert_fusion
  199.4 0.5 fusion.18
  200.1 18.1 %reshape.809 = f32[4,2,32,2,64,2]{5,4,3,2,1,0:T(8,128)} reshape(f32[1,8,64,128]{3,2,1,0:T(8,128)S(1)} %copy.140) | data formatting | bytes 524288 | tf_op jit(solution)/shard_map/reshape | solution.py:48
  218.2 7.0 %reduce_sum.60 = f32[4,32,64]{2,1,0:T(8,128)S(1)} reduce(f32[4,2,32,2,64,2]{5,4,3,2,1,0:T(8,128)} %reshape.809, f32[]{:T(128)} %constant.51.clone.1), dimensions={1,3,5}, to_apply=%region_4.5 | reduce | flops 57344 | bytes 294916 | tf_op jit(solution)/shard_map/reduce_sum | solution.py:49
  225.4 1.9 collective-permute-start.4
  227.3 7.6 %collective-permute-start.5 = (bf16[1,1,32,64]{3,2,1,0:T(8,128)(2,1)S(1)}, bf16[1,1,32,64]{3,2,1,0:T(8,128)(2,1)S(1)}, u32[]{:S(2)}, u32[]{:S(2)}) collective-permute-start(bf16[1,1,32,64]{3,2,1,0:T(8,128)(2,1)S(1)} %get-tuple-element.91), channel_id=1, source_target_pairs={{8,0},{16,8},{24,16},{32,24},{40,32},{48,40},{56,48},{64,56},{72,6... | collective-permute-start | bytes 12296 | tf_op jit(solution)/shard_map/ppermute | solution.py:24
  235.0 1.3 collective-permute-done.5
  236.4 2.1 reshape.810
  238.6 0.2 reduce_sum.61
  239.0 1.9 collective-permute-start.6
  240.9 7.5 %collective-permute-start.7 = (bf16[1,1,16,32]{3,2,1,0:T(8,128)(2,1)S(1)}, bf16[1,1,16,32]{3,2,1,0:T(8,128)(2,1)S(1)}, u32[]{:S(2)}, u32[]{:S(2)}) collective-permute-start(bf16[1,1,16,32]{3,2,1,0:T(8,128)(2,1)S(1)} %get-tuple-element.116), channel_id=1, source_target_pairs={{8,0},{16,8},{24,16},{32,24},{40,32},{48,40},{56,48},{64,56},{72,6... | collective-permute-start | bytes 3080 | tf_op jit(solution)/shard_map/ppermute | solution.py:24
  248.5 1.3 collective-permute-done.7
  250.2 7.5 %collective-permute-start.9 = (bf16[1,1,8,16]{3,2,1,0:T(8,128)(2,1)S(1)}, bf16[1,1,8,16]{3,2,1,0:T(8,128)(2,1)S(1)}, u32[]{:S(2)}, u32[]{:S(2)}) collective-permute-start(bf16[1,1,8,16]{3,2,1,0:T(8,128)(2,1)S(1)} %get-tuple-element.126), channel_id=1, source_target_pairs={{8,0},{16,8},{24,16},{32,24},{40,32},{48,40},{56,48},{64,56},{72,6... | collective-permute-start | bytes 776 | tf_op jit(solution)/shard_map/ppermute | solution.py:24
  257.7 1.9 collective-permute-start.8
  259.7 6.8 %collective-permute-done.8 = bf16[1,1,8,16]{3,2,1,0:T(8,128)(2,1)S(1)} collective-permute-done((bf16[1,1,8,16]{3,2,1,0:T(8,128)(2,1)S(1)}, bf16[1,1,8,16]{3,2,1,0:T(8,128)(2,1)S(1)}, u32[]{:S(2)}, u32[]{:S(2)}) %collective-permute-start.8) | collective-permute-done | bytes 288 | tf_op jit(solution)/shard_map/ppermute | solution.py:21
  266.7 1.9 collective-permute-start.11
  268.7 3.9 collective-permute-start.10
  272.6 4.8 collective-permute-done.10
  277.9 1.9 collective-permute-start.12
  279.8 7.2 %collective-permute-start.13 = (bf16[1,1,16,32]{3,2,1,0:T(8,128)(2,1)S(1)}, bf16[1,1,16,32]{3,2,1,0:T(8,128)(2,1)S(1)}, u32[]{:S(2)}, u32[]{:S(2)}) collective-permute-start(bf16[1,1,16,32]{3,2,1,0:T(8,128)(2,1)S(1)} %get-tuple-element.114), channel_id=1, source_target_pairs={{8,0},{16,8},{24,16},{32,24},{40,32},{48,40},{56,48},{64,56},{72,6... | collective-permute-start | bytes 3080 | tf_op jit(solution)/shard_map/ppermute | solution.py:24
  287.1 1.3 collective-permute-done.13
  289.0 1.9 collective-permute-start.14
  290.9 7.5 %collective-permute-start.15 = (bf16[1,1,32,64]{3,2,1,0:T(8,128)(2,1)S(1)}, bf16[1,1,32,64]{3,2,1,0:T(8,128)(2,1)S(1)}, u32[]{:S(2)}, u32[]{:S(2)}) collective-permute-start(bf16[1,1,32,64]{3,2,1,0:T(8,128)(2,1)S(1)} %get-tuple-element.89), channel_id=1, source_target_pairs={{8,0},{16,8},{24,16},{32,24},{40,32},{48,40},{56,48},{64,56},{72,6... | collective-permute-start | bytes 12296 | tf_op jit(solution)/shard_map/ppermute | solution.py:24
  298.5 1.2 collective-permute-done.15
  300.9 1.9 collective-permute-start.16
  302.8 7.7 %collective-permute-start.17 = (bf16[1,1,64,128]{2,1,3,0:T(2,128)(2,1)S(1)}, bf16[1,1,64,128]{2,1,3,0:T(2,128)(2,1)S(1)}, u32[]{:S(2)}, u32[]{:S(2)}) collective-permute-start(bf16[1,1,64,128]{2,1,3,0:T(2,128)(2,1)S(1)} %get-tuple-element.57), channel_id=1, source_target_pairs={{8,0},{16,8},{24,16},{32,24},{40,32},{48,40},{56,48},{64,56},{72,6... | collective-permute-start | bytes 49160 | tf_op jit(solution)/shard_map/ppermute | solution.py:24
  310.6 1.8 collective-permute-done.17
  312.4 0.3 maximum_convert_fusion.1
  312.7 0.6 fusion.97
  313.5 0.8 reshape.813
  314.4 25.8 %all-gather.3.cloned.1.call-done = bf16[8,1,65536]{2,1,0:T(2,128)(2,1)} async-done(((bf16[1,1,65536]{2,1,0:T(2,128)(2,1)}), bf16[8,1,65536]{2,1,0:T(2,128)(2,1)}) %all-gather.3.cloned.1.call-update) | async-done | bytes 1048592 | tf_op jit(solution)/shard_map/all_gather | solution.py:101
  340.2 2.9 fusion
  343.1 0.9 copy.151
  344.0 144.2 %psum.23 = f32[1,8]{1,0:T(1,128)S(1)} all-reduce(f32[1,8]{1,0:T(1,128)S(1)} %fusion), channel_id=1, replica_groups=mesh['grid'=64,'state'=8] {'grid'}, use_global_device_ids=true, to_apply=%region_8.9 | all-reduce | flops 8 | bytes 64 | tf_op jit(solution)/shard_map/psum | solution.py:104
  488.2 0.5 broadcast_multiply_fusion.1
  (99 shorter events, 4.6 us)
Async XLA Ops:
  7.2 333.0 %all-gather.3.cloned.1.call-start = ((), (), s32[]{:S(2)}) async-start(), calls=%async_computation | async-start | bytes 2359296 | tf_op jit(solution)/shard_map/all_gather | solution.py:101
  8.7 25.6 %collective-permute-start.1 = (f32[1,2,64,128]{3,2,1,0:T(8,128)S(1)}, f32[1,2,64,128]{3,2,1,0:T(8,128)S(1)}, u32[]{:S(2)}, u32[]{:S(2)}) collective-permute-start(f32[1,2,64,128]{3,2,1,0:T(8,128)S(1)} %get-tuple-element.63), channel_id=1, source_target_pairs={{0,8},{8,16},{16,24},{24,32},{32,40},{40,48},{48,56},{56,64},{64,7... | collective-permute-start | bytes 196616 | tf_op jit(solution)/shard_map/ppermute | solution.py:21
  12.5 23.6 %collective-permute-start = (f32[1,2,64,128]{3,2,1,0:T(8,128)}, f32[1,2,64,128]{3,2,1,0:T(8,128)S(1)}, u32[]{:S(2)}, u32[]{:S(2)}) collective-permute-start(f32[1,2,64,128]{3,2,1,0:T(8,128)} %get-tuple-element.64), channel_id=1, source_target_pairs={{8,0},{16,8},{24,16},{32,24},{40,32},{48,40},{56,48},{64,56},{72,6... | collective-permute-start | bytes 196616 | tf_op jit(solution)/shard_map/ppermute | solution.py:24
  30.5 2.8 copy-start.1
  30.5 3.8 copy-start
  36.1 4.8 copy-start.2
  36.1 4.8 copy-start.3
  188.0 9.5 %collective-permute-start.2 = (bf16[1,1,64,128]{2,1,3,0:T(2,128)(2,1)S(1)}, bf16[1,1,64,128]{2,1,3,0:T(2,128)(2,1)S(1)}, u32[]{:S(2)}, u32[]{:S(2)}) collective-permute-start(bf16[1,1,64,128]{2,1,3,0:T(2,128)(2,1)S(1)} %get-tuple-element.58), channel_id=1, source_target_pairs={{0,8},{8,16},{16,24},{24,32},{32,40},{40,48},{48,56},{56,64},{64,7... | collective-permute-start | bytes 49160 | tf_op jit(solution)/shard_map/ppermute | solution.py:21
  190.0 9.1 %collective-permute-start.3 = (bf16[1,1,64,128]{2,1,3,0:T(2,128)(2,1)S(1)}, bf16[1,1,64,128]{2,1,3,0:T(2,128)(2,1)S(1)}, u32[]{:S(2)}, u32[]{:S(2)}) collective-permute-start(bf16[1,1,64,128]{2,1,3,0:T(2,128)(2,1)S(1)} %get-tuple-element.59), channel_id=1, source_target_pairs={{8,0},{16,8},{24,16},{32,24},{40,32},{48,40},{56,48},{64,56},{72,6... | collective-permute-start | bytes 49160 | tf_op jit(solution)/shard_map/ppermute | solution.py:24
  225.4 9.5 %collective-permute-start.4 = (bf16[1,1,32,64]{3,2,1,0:T(8,128)(2,1)S(1)}, bf16[1,1,32,64]{3,2,1,0:T(8,128)(2,1)S(1)}, u32[]{:S(2)}, u32[]{:S(2)}) collective-permute-start(bf16[1,1,32,64]{3,2,1,0:T(8,128)(2,1)S(1)} %get-tuple-element.90), channel_id=1, source_target_pairs={{0,8},{8,16},{16,24},{24,32},{32,40},{40,48},{48,56},{56,64},{64,7... | collective-permute-start | bytes 12296 | tf_op jit(solution)/shard_map/ppermute | solution.py:21
  227.3 8.9 %collective-permute-start.5 = (bf16[1,1,32,64]{3,2,1,0:T(8,128)(2,1)S(1)}, bf16[1,1,32,64]{3,2,1,0:T(8,128)(2,1)S(1)}, u32[]{:S(2)}, u32[]{:S(2)}) collective-permute-start(bf16[1,1,32,64]{3,2,1,0:T(8,128)(2,1)S(1)} %get-tuple-element.91), channel_id=1, source_target_pairs={{8,0},{16,8},{24,16},{32,24},{40,32},{48,40},{56,48},{64,56},{72,6... | collective-permute-start | bytes 12296 | tf_op jit(solution)/shard_map/ppermute | solution.py:24
  239.0 9.5 %collective-permute-start.6 = (bf16[1,1,16,32]{3,2,1,0:T(8,128)(2,1)S(1)}, bf16[1,1,16,32]{3,2,1,0:T(8,128)(2,1)S(1)}, u32[]{:S(2)}, u32[]{:S(2)}) collective-permute-start(bf16[1,1,16,32]{3,2,1,0:T(8,128)(2,1)S(1)} %get-tuple-element.115), channel_id=1, source_target_pairs={{0,8},{8,16},{16,24},{24,32},{32,40},{40,48},{48,56},{56,64},{64,7... | collective-permute-start | bytes 3080 | tf_op jit(solution)/shard_map/ppermute | solution.py:21
  240.9 8.8 %collective-permute-start.7 = (bf16[1,1,16,32]{3,2,1,0:T(8,128)(2,1)S(1)}, bf16[1,1,16,32]{3,2,1,0:T(8,128)(2,1)S(1)}, u32[]{:S(2)}, u32[]{:S(2)}) collective-permute-start(bf16[1,1,16,32]{3,2,1,0:T(8,128)(2,1)S(1)} %get-tuple-element.116), channel_id=1, source_target_pairs={{8,0},{16,8},{24,16},{32,24},{40,32},{48,40},{56,48},{64,56},{72,6... | collective-permute-start | bytes 3080 | tf_op jit(solution)/shard_map/ppermute | solution.py:24
  250.2 9.4 %collective-permute-start.9 = (bf16[1,1,8,16]{3,2,1,0:T(8,128)(2,1)S(1)}, bf16[1,1,8,16]{3,2,1,0:T(8,128)(2,1)S(1)}, u32[]{:S(2)}, u32[]{:S(2)}) collective-permute-start(bf16[1,1,8,16]{3,2,1,0:T(8,128)(2,1)S(1)} %get-tuple-element.126), channel_id=1, source_target_pairs={{8,0},{16,8},{24,16},{32,24},{40,32},{48,40},{56,48},{64,56},{72,6... | collective-permute-start | bytes 776 | tf_op jit(solution)/shard_map/ppermute | solution.py:24
  257.7 8.8 %collective-permute-start.8 = (bf16[1,1,8,16]{3,2,1,0:T(8,128)(2,1)S(1)}, bf16[1,1,8,16]{3,2,1,0:T(8,128)(2,1)S(1)}, u32[]{:S(2)}, u32[]{:S(2)}) collective-permute-start(bf16[1,1,8,16]{3,2,1,0:T(8,128)(2,1)S(1)} %get-tuple-element.126), channel_id=1, source_target_pairs={{0,8},{8,16},{16,24},{24,32},{32,40},{40,48},{48,56},{56,64},{64,7... | collective-permute-start | bytes 776 | tf_op jit(solution)/shard_map/ppermute | solution.py:21
  266.7 5.9 %collective-permute-start.11 = (bf16[1,1,8,16]{3,2,1,0:T(8,128)(2,1)S(1)}, bf16[1,1,8,16]{3,2,1,0:T(8,128)(2,1)S(1)}, u32[]{:S(2)}, u32[]{:S(2)}) collective-permute-start(bf16[1,1,8,16]{3,2,1,0:T(8,128)(2,1)S(1)} %get-tuple-element.16), channel_id=1, source_target_pairs={{8,0},{16,8},{24,16},{32,24},{40,32},{48,40},{56,48},{64,56},{72,6... | collective-permute-start | bytes 776 | tf_op jit(solution)/shard_map/ppermute | solution.py:24
  268.7 8.8 %collective-permute-start.10 = (bf16[1,1,8,16]{3,2,1,0:T(8,128)(2,1)S(1)}, bf16[1,1,8,16]{3,2,1,0:T(8,128)(2,1)S(1)}, u32[]{:S(2)}, u32[]{:S(2)}) collective-permute-start(bf16[1,1,8,16]{3,2,1,0:T(8,128)(2,1)S(1)} %get-tuple-element.16), channel_id=1, source_target_pairs={{0,8},{8,16},{16,24},{24,32},{32,40},{40,48},{48,56},{56,64},{64,7... | collective-permute-start | bytes 776 | tf_op jit(solution)/shard_map/ppermute | solution.py:21
  277.9 9.2 %collective-permute-start.12 = (bf16[1,1,16,32]{3,2,1,0:T(8,128)(2,1)S(1)}, bf16[1,1,16,32]{3,2,1,0:T(8,128)(2,1)S(1)}, u32[]{:S(2)}, u32[]{:S(2)}) collective-permute-start(bf16[1,1,16,32]{3,2,1,0:T(8,128)(2,1)S(1)} %get-tuple-element.113), channel_id=1, source_target_pairs={{0,8},{8,16},{16,24},{24,32},{32,40},{40,48},{48,56},{56,64},{64,7... | collective-permute-start | bytes 3080 | tf_op jit(solution)/shard_map/ppermute | solution.py:21
  279.8 8.6 %collective-permute-start.13 = (bf16[1,1,16,32]{3,2,1,0:T(8,128)(2,1)S(1)}, bf16[1,1,16,32]{3,2,1,0:T(8,128)(2,1)S(1)}, u32[]{:S(2)}, u32[]{:S(2)}) collective-permute-start(bf16[1,1,16,32]{3,2,1,0:T(8,128)(2,1)S(1)} %get-tuple-element.114), channel_id=1, source_target_pairs={{8,0},{16,8},{24,16},{32,24},{40,32},{48,40},{56,48},{64,56},{72,6... | collective-permute-start | bytes 3080 | tf_op jit(solution)/shard_map/ppermute | solution.py:24
  289.0 9.6 %collective-permute-start.14 = (bf16[1,1,32,64]{3,2,1,0:T(8,128)(2,1)S(1)}, bf16[1,1,32,64]{3,2,1,0:T(8,128)(2,1)S(1)}, u32[]{:S(2)}, u32[]{:S(2)}) collective-permute-start(bf16[1,1,32,64]{3,2,1,0:T(8,128)(2,1)S(1)} %get-tuple-element.88), channel_id=1, source_target_pairs={{0,8},{8,16},{16,24},{24,32},{32,40},{40,48},{48,56},{56,64},{64,7... | collective-permute-start | bytes 12296 | tf_op jit(solution)/shard_map/ppermute | solution.py:21
  290.9 8.9 %collective-permute-start.15 = (bf16[1,1,32,64]{3,2,1,0:T(8,128)(2,1)S(1)}, bf16[1,1,32,64]{3,2,1,0:T(8,128)(2,1)S(1)}, u32[]{:S(2)}, u32[]{:S(2)}) collective-permute-start(bf16[1,1,32,64]{3,2,1,0:T(8,128)(2,1)S(1)} %get-tuple-element.89), channel_id=1, source_target_pairs={{8,0},{16,8},{24,16},{32,24},{40,32},{48,40},{56,48},{64,56},{72,6... | collective-permute-start | bytes 12296 | tf_op jit(solution)/shard_map/ppermute | solution.py:24
  300.9 9.8 %collective-permute-start.16 = (bf16[1,1,64,128]{2,1,3,0:T(2,128)(2,1)S(1)}, bf16[1,1,64,128]{2,1,3,0:T(2,128)(2,1)S(1)}, u32[]{:S(2)}, u32[]{:S(2)}) collective-permute-start(bf16[1,1,64,128]{2,1,3,0:T(2,128)(2,1)S(1)} %get-tuple-element.56), channel_id=1, source_target_pairs={{0,8},{8,16},{16,24},{24,32},{32,40},{40,48},{48,56},{56,64},{64,7... | collective-permute-start | bytes 49160 | tf_op jit(solution)/shard_map/ppermute | solution.py:21
  302.8 9.6 %collective-permute-start.17 = (bf16[1,1,64,128]{2,1,3,0:T(2,128)(2,1)S(1)}, bf16[1,1,64,128]{2,1,3,0:T(2,128)(2,1)S(1)}, u32[]{:S(2)}, u32[]{:S(2)}) collective-permute-start(bf16[1,1,64,128]{2,1,3,0:T(2,128)(2,1)S(1)} %get-tuple-element.57), channel_id=1, source_target_pairs={{8,0},{16,8},{24,16},{32,24},{40,32},{48,40},{56,48},{64,56},{72,6... | collective-permute-start | bytes 49160 | tf_op jit(solution)/shard_map/ppermute | solution.py:24
Sparse Core Ops, SparseCore 0:
  314.4 25.7 all-gather.2
where the time goes:
time: 496 us
  blocking collectives  285 us (57%)
  starting transfers between devices  87.3 us (18%)
  waiting for transfers between devices  46.3 us (9%)
  local copies, waits for them, and re-layouts  42.6 us (9%)
  between operations  16 us (3%)
  other arithmetic  15.5 us (3%)
    psum x1, blocking collectives, on_device(): summed = lax.psum(row_block, 'grid')  144 us
    psum x1, blocking collectives, on_device(): lax.psum((jnp.sum(orbitals * hpsi, axis=(1, 2, 3)), jnp.sum(orbitals * or...  141 us
    ppermute x9, starting transfers between devices, with_halo(): lax.ppermute(lax.slice_in_dim(block, 0, width, axis=dim), axis, backward)  66.1 us
    all_gather x1, waiting for transfers between devices, on_device(): lax.all_gather(rounded, 'state', axis=0, tiled=True)  25.8 us
    ppermute x9, starting transfers between devices, with_halo(): lax.ppermute(lax.slice_in_dim(block, block.shape[dim] - width, None, axis...  21.2 us
    reshape x2, local copies, waits for them, and re-layouts, restrict(): shaped = values.reshape(count, sx // 2, 2, sy // 2, 2, sz // 2, 2)  20.2 us
    ppermute x9, waiting for transfers between devices, with_halo(): lax.ppermute(lax.slice_in_dim(block, block.shape[dim] - width, None, axis...  12.1 us
  transfers between devices with their start and end apart: 19, of which 11 were waited for; matrix products, arithmetic and copies ran while one was open for 2% of the time, Pallas kernels for 0%

commit v1 on v0

--- a/solution.py
+++ b/solution.py
@@ -98,7 +98,9 @@
     row_block = jnp.einsum(
         "ac,bc->ab",
         rounded,
-        lax.all_gather(rounded, "state", axis=0, tiled=True),
+        jnp.concatenate(
+            lax.all_to_all(jnp.stack([rounded] * lax.axis_size("state")), "state", 0, 0), axis=0
+        ),
         preferred_element_type=jnp.float32,
     )
     summed = lax.psum(row_block, "grid")

time: 496 us -> 479 us (0.966)
  the two profiles are of different devices: /device:TPU:4 before, /device:TPU:2 now
where the time goes in v1:
time: 479 us; the launch traced here: 478 us
  blocking collectives  284 us (59%)
  starting transfers between devices  96 us (20%)
  local copies, waits for them, and re-layouts  45.2 us (9%)
  waiting for transfers between devices  25.4 us (5%)
  other arithmetic  23.3 us (5%)
    psum x1, blocking collectives, on_device(): summed = lax.psum(row_block, 'grid')  144 us
    psum x1, blocking collectives, on_device(): lax.psum((jnp.sum(orbitals * hpsi, axis=(1, 2, 3)), jnp.sum(orbitals * or...  141 us
    ppermute x9, starting transfers between devices, with_halo(): lax.ppermute(lax.slice_in_dim(block, 0, width, axis=dim), axis, backward)  72 us
    reshape x2, local copies, waits for them, and re-layouts, restrict(): shaped = values.reshape(count, sx // 2, 2, sy // 2, 2, sz // 2, 2)  20.2 us
    ppermute x9, starting transfers between devices, with_halo(): lax.ppermute(lax.slice_in_dim(block, block.shape[dim] - width, None, axis...  19.2 us
    all_to_all x1, waiting for transfers between devices, on_device(): lax.all_to_all(jnp.stack([rounded] * lax.axis_size('state')), 'state', 0, 0)  14.3 us
    unnamed x20, local copies, waits for them, and re-layouts  12.7 us
    ppermute x9, waiting for transfers between devices, with_halo(): lax.ppermute(lax.slice_in_dim(block, 0, width, axis=dim), axis, backward)  10.6 us
  transfers between devices with their start and end apart: 19, of which 11 were waited for; matrix products, arithmetic and copies ran while one was open for 2% of the time, Pallas kernels for 0%

profile of v1, /device:TPU:2, one launch (start us, length us, event | category | flops | bytes accessed | tf_op | source)
XLA Modules:
  0.0 478.1 jit_solution(10366700870898314755)
XLA Ops:
  0.6 0.9 fusion.122
  1.5 3.8 collective-permute-start.1
  5.4 11.9 %collective-permute-start = (f32[1,2,64,128]{3,2,1,0:T(8,128)S(1)}, f32[1,2,64,128]{3,2,1,0:T(8,128)S(1)}, u32[]{:S(2)}, u32[]{:S(2)}) collective-permute-start(f32[1,2,64,128]{3,2,1,0:T(8,128)S(1)} %get-tuple-element.64), channel_id=1, source_target_pairs={{8,0},{16,8},{24,16},{32,24},{40,32},{48,40},{56,48},{64,56},{72,6... | collective-permute-start | bytes 196616 | tf_op jit(solution)/shard_map/ppermute | solution.py:24
  17.3 1.2 copy.113
  18.5 1.1 fusion.112
  19.6 1.1 fusion.113
  20.7 1.0 fusion.115
  21.8 1.0 fusion.117
  22.8 0.3 copy.123
  23.1 0.3 copy.125
  23.4 0.3 copy.119
  23.9 1.0 copy.134
  24.9 0.7 multiply_reduce_fusion.1
  25.6 0.7 copy-done.2
  26.4 0.9 fusion.119
  27.2 1.9 copy.150
  29.2 1.9 copy.152
  31.2 1.0 copy.151
  32.2 1.0 copy.153
  33.2 4.4 multiply_reduce_fusion
  37.6 140.7 %all-reduce = (f32[1]{0:T(128)}, f32[1]{0:T(128)}) all-reduce(f32[1]{0:T(128)} %bitcast.1, f32[1]{0:T(128)} %bitcast.2), channel_id=1, replica_groups=mesh['grid'=64,'state'=8] {'grid'}, use_global_device_ids=true, to_apply=%region_1.2 | all-reduce | flops 2 | bytes 16 | tf_op jit(solution)/shard_map/psum | solution.py:89
  180.3 1.9 collective-permute-start.2
  182.2 7.2 %collective-permute-start.3 = (bf16[1,1,64,128]{2,1,3,0:T(2,128)(2,1)S(1)}, bf16[1,1,64,128]{2,1,3,0:T(2,128)(2,1)S(1)}, u32[]{:S(2)}, u32[]{:S(2)}) collective-permute-start(bf16[1,1,64,128]{2,1,3,0:T(2,128)(2,1)S(1)} %get-tuple-element.59), channel_id=1, source_target_pairs={{8,0},{16,8},{24,16},{32,24},{40,32},{48,40},{56,48},{64,56},{72,6... | collective-permute-start | bytes 49160 | tf_op jit(solution)/shard_map/ppermute | solution.py:24
  189.5 0.3 collective-permute-done.2
  189.8 1.6 collective-permute-done.3
  191.4 0.3 maximum_convert_fusion
  191.7 0.5 fusion.18
  192.4 18.1 %reshape.814 = f32[4,2,32,2,64,2]{5,4,3,2,1,0:T(8,128)} reshape(f32[1,8,64,128]{3,2,1,0:T(8,128)S(1)} %copy.138) | data formatting | bytes 524288 | tf_op jit(solution)/shard_map/reshape | solution.py:48
  210.5 7.0 %reduce_sum.60 = f32[4,32,64]{2,1,0:T(8,128)S(1)} reduce(f32[4,2,32,2,64,2]{5,4,3,2,1,0:T(8,128)} %reshape.814, f32[]{:T(128)} %constant.51.clone.1), dimensions={1,3,5}, to_apply=%region_4.5 | reduce | flops 57344 | bytes 294916 | tf_op jit(solution)/shard_map/reduce_sum | solution.py:49
  217.7 1.9 collective-permute-start.4
  219.6 7.6 %collective-permute-start.5 = (bf16[1,1,32,64]{3,2,1,0:T(8,128)(2,1)S(1)}, bf16[1,1,32,64]{3,2,1,0:T(8,128)(2,1)S(1)}, u32[]{:S(2)}, u32[]{:S(2)}) collective-permute-start(bf16[1,1,32,64]{3,2,1,0:T(8,128)(2,1)S(1)} %get-tuple-element.91), channel_id=1, source_target_pairs={{8,0},{16,8},{24,16},{32,24},{40,32},{48,40},{56,48},{64,56},{72,6... | collective-permute-start | bytes 12296 | tf_op jit(solution)/shard_map/ppermute | solution.py:24
  227.2 1.3 collective-permute-done.5
  228.7 2.2 reshape.815
  231.2 1.9 collective-permute-start.6
  233.2 7.5 %collective-permute-start.7 = (bf16[1,1,16,32]{3,2,1,0:T(8,128)(2,1)S(1)}, bf16[1,1,16,32]{3,2,1,0:T(8,128)(2,1)S(1)}, u32[]{:S(2)}, u32[]{:S(2)}) collective-permute-start(bf16[1,1,16,32]{3,2,1,0:T(8,128)(2,1)S(1)} %get-tuple-element.116), channel_id=1, source_target_pairs={{8,0},{16,8},{24,16},{32,24},{40,32},{48,40},{56,48},{64,56},{72,6... | collective-permute-start | bytes 3080 | tf_op jit(solution)/shard_map/ppermute | solution.py:24
  240.7 1.3 collective-permute-done.7
  242.3 1.9 collective-permute-start.8
  244.2 7.5 %collective-permute-start.9 = (bf16[1,1,8,16]{3,2,1,0:T(8,128)(2,1)S(1)}, bf16[1,1,8,16]{3,2,1,0:T(8,128)(2,1)S(1)}, u32[]{:S(2)}, u32[]{:S(2)}) collective-permute-start(bf16[1,1,8,16]{3,2,1,0:T(8,128)(2,1)S(1)} %get-tuple-element.126), channel_id=1, source_target_pairs={{8,0},{16,8},{24,16},{32,24},{40,32},{48,40},{56,48},{64,56},{72,6... | collective-permute-start | bytes 776 | tf_op jit(solution)/shard_map/ppermute | solution.py:24
  251.9 1.1 collective-permute-done.9
  253.1 1.9 collective-permute-start.10
  255.0 7.5 %collective-permute-start.11 = (bf16[1,1,8,16]{3,2,1,0:T(8,128)(2,1)S(1)}, bf16[1,1,8,16]{3,2,1,0:T(8,128)(2,1)S(1)}, u32[]{:S(2)}, u32[]{:S(2)}) collective-permute-start(bf16[1,1,8,16]{3,2,1,0:T(8,128)(2,1)S(1)} %get-tuple-element.16), channel_id=1, source_target_pairs={{8,0},{16,8},{24,16},{32,24},{40,32},{48,40},{56,48},{64,56},{72,6... | collective-permute-start | bytes 776 | tf_op jit(solution)/shard_map/ppermute | solution.py:24
  262.7 1.1 collective-permute-done.11
  264.3 1.9 collective-permute-start.12
  266.2 7.5 %collective-permute-start.13 = (bf16[1,1,16,32]{3,2,1,0:T(8,128)(2,1)S(1)}, bf16[1,1,16,32]{3,2,1,0:T(8,128)(2,1)S(1)}, u32[]{:S(2)}, u32[]{:S(2)}) collective-permute-start(bf16[1,1,16,32]{3,2,1,0:T(8,128)(2,1)S(1)} %get-tuple-element.114), channel_id=1, source_target_pairs={{8,0},{16,8},{24,16},{32,24},{40,32},{48,40},{56,48},{64,56},{72,6... | collective-permute-start | bytes 3080 | tf_op jit(solution)/shard_map/ppermute | solution.py:24
  273.7 1.3 collective-permute-done.13
  275.7 1.9 collective-permute-start.14
  277.6 7.5 %collective-permute-start.15 = (bf16[1,1,32,64]{3,2,1,0:T(8,128)(2,1)S(1)}, bf16[1,1,32,64]{3,2,1,0:T(8,128)(2,1)S(1)}, u32[]{:S(2)}, u32[]{:S(2)}) collective-permute-start(bf16[1,1,32,64]{3,2,1,0:T(8,128)(2,1)S(1)} %get-tuple-element.89), channel_id=1, source_target_pairs={{8,0},{16,8},{24,16},{32,24},{40,32},{48,40},{56,48},{64,56},{72,6... | collective-permute-start | bytes 12296 | tf_op jit(solution)/shard_map/ppermute | solution.py:24
  285.2 1.3 collective-permute-done.15
  287.6 1.9 collective-permute-start.16
  289.5 7.7 %collective-permute-start.17 = (bf16[1,1,64,128]{2,1,3,0:T(2,128)(2,1)S(1)}, bf16[1,1,64,128]{2,1,3,0:T(2,128)(2,1)S(1)}, u32[]{:S(2)}, u32[]{:S(2)}) collective-permute-start(bf16[1,1,64,128]{2,1,3,0:T(2,128)(2,1)S(1)} %get-tuple-element.57), channel_id=1, source_target_pairs={{8,0},{16,8},{24,16},{32,24},{40,32},{48,40},{56,48},{64,56},{72,6... | collective-permute-start | bytes 49160 | tf_op jit(solution)/shard_map/ppermute | solution.py:24
  297.4 1.6 collective-permute-done.17
  298.9 0.3 maximum_convert_fusion.1
  299.3 1.4 fusion.97
  300.8 1.1 stack.3
  301.9 0.5 broadcast.366
  302.4 7.0 %reduce.7 = bf16[8,65536]{1,0:T(8,128)(2,1)S(1)} reduce(bf16[8,1,65536]{2,1,0:T(2,128)(2,1)S(1)} %stack.3, bf16[]{:T(256)} %broadcast.366), dimensions={1}, to_apply=%stack.3.reduce_sub_computation | reduce | bytes 2097154 | tf_op jit(solution)/shard_map/stack | solution.py:102
  309.5 1.9 reshape.820
  311.4 4.8 %all-to-all-start = ((bf16[8,2,32768]{2,1,0:T(2,128)(2,1)}), bf16[8,2,32768]{2,1,0:T(2,128)(2,1)S(1)}, u32[]{:S(2)}, u32[]{:S(2)}) async-start(bf16[8,2,32768]{2,1,0:T(2,128)(2,1)} %reshape.820), calls=%async_computation | async-start | bytes 2097152 | tf_op jit(solution)/shard_map/all_to_all | solution.py:102
  316.3 14.3 %all-to-all-done = bf16[8,2,32768]{2,1,0:T(2,128)(2,1)S(1)} async-done(((bf16[8,2,32768]{2,1,0:T(2,128)(2,1)}), bf16[8,2,32768]{2,1,0:T(2,128)(2,1)S(1)}, u32[]{:S(2)}, u32[]{:S(2)}) %all-to-all-start) | async-done | bytes 1048608 | tf_op jit(solution)/shard_map/all_to_all | solution.py:102
  330.7 1.0 reshape.821
  331.7 1.3 fusion
  333.1 0.9 copy.148
  334.0 143.6 %psum.23 = f32[1,8]{1,0:T(1,128)S(1)} all-reduce(f32[1,8]{1,0:T(1,128)S(1)} %fusion), channel_id=1, replica_groups=mesh['grid'=64,'state'=8] {'grid'}, use_global_device_ids=true, to_apply=%region_8.9 | all-reduce | flops 8 | bytes 64 | tf_op jit(solution)/shard_map/psum | solution.py:106
  477.6 0.5 broadcast_multiply_fusion.1
  (104 shorter events, 5.2 us)
Async XLA Ops:
  1.5 23.4 %collective-permute-start.1 = (f32[1,2,64,128]{3,2,1,0:T(8,128)S(1)}, f32[1,2,64,128]{3,2,1,0:T(8,128)S(1)}, u32[]{:S(2)}, u32[]{:S(2)}) collective-permute-start(f32[1,2,64,128]{3,2,1,0:T(8,128)S(1)} %get-tuple-element.63), channel_id=1, source_target_pairs={{0,8},{8,16},{16,24},{24,32},{32,40},{40,48},{48,56},{56,64},{64,7... | collective-permute-start | bytes 196616 | tf_op jit(solution)/shard_map/ppermute | solution.py:21
  5.4 20.3 %collective-permute-start = (f32[1,2,64,128]{3,2,1,0:T(8,128)S(1)}, f32[1,2,64,128]{3,2,1,0:T(8,128)S(1)}, u32[]{:S(2)}, u32[]{:S(2)}) collective-permute-start(f32[1,2,64,128]{3,2,1,0:T(8,128)S(1)} %get-tuple-element.64), channel_id=1, source_target_pairs={{8,0},{16,8},{24,16},{32,24},{40,32},{48,40},{56,48},{64,56},{72,6... | collective-permute-start | bytes 196616 | tf_op jit(solution)/shard_map/ppermute | solution.py:24
  20.7 2.1 copy-start.1
  21.8 2.1 copy-start.4
  25.6 0.7 copy-start.2
  26.4 4.8 copy-start.3
  180.3 9.5 %collective-permute-start.2 = (bf16[1,1,64,128]{2,1,3,0:T(2,128)(2,1)S(1)}, bf16[1,1,64,128]{2,1,3,0:T(2,128)(2,1)S(1)}, u32[]{:S(2)}, u32[]{:S(2)}) collective-permute-start(bf16[1,1,64,128]{2,1,3,0:T(2,128)(2,1)S(1)} %get-tuple-element.58), channel_id=1, source_target_pairs={{0,8},{8,16},{16,24},{24,32},{32,40},{40,48},{48,56},{56,64},{64,7... | collective-permute-start | bytes 49160 | tf_op jit(solution)/shard_map/ppermute | solution.py:21
  182.2 9.1 %collective-permute-start.3 = (bf16[1,1,64,128]{2,1,3,0:T(2,128)(2,1)S(1)}, bf16[1,1,64,128]{2,1,3,0:T(2,128)(2,1)S(1)}, u32[]{:S(2)}, u32[]{:S(2)}) collective-permute-start(bf16[1,1,64,128]{2,1,3,0:T(2,128)(2,1)S(1)} %get-tuple-element.59), channel_id=1, source_target_pairs={{8,0},{16,8},{24,16},{32,24},{40,32},{48,40},{56,48},{64,56},{72,6... | collective-permute-start | bytes 49160 | tf_op jit(solution)/shard_map/ppermute | solution.py:24
  217.7 9.5 %collective-permute-start.4 = (bf16[1,1,32,64]{3,2,1,0:T(8,128)(2,1)S(1)}, bf16[1,1,32,64]{3,2,1,0:T(8,128)(2,1)S(1)}, u32[]{:S(2)}, u32[]{:S(2)}) collective-permute-start(bf16[1,1,32,64]{3,2,1,0:T(8,128)(2,1)S(1)} %get-tuple-element.90), channel_id=1, source_target_pairs={{0,8},{8,16},{16,24},{24,32},{32,40},{40,48},{48,56},{56,64},{64,7... | collective-permute-start | bytes 12296 | tf_op jit(solution)/shard_map/ppermute | solution.py:21
  219.6 8.9 %collective-permute-start.5 = (bf16[1,1,32,64]{3,2,1,0:T(8,128)(2,1)S(1)}, bf16[1,1,32,64]{3,2,1,0:T(8,128)(2,1)S(1)}, u32[]{:S(2)}, u32[]{:S(2)}) collective-permute-start(bf16[1,1,32,64]{3,2,1,0:T(8,128)(2,1)S(1)} %get-tuple-element.91), channel_id=1, source_target_pairs={{8,0},{16,8},{24,16},{32,24},{40,32},{48,40},{56,48},{64,56},{72,6... | collective-permute-start | bytes 12296 | tf_op jit(solution)/shard_map/ppermute | solution.py:24
  231.2 9.5 %collective-permute-start.6 = (bf16[1,1,16,32]{3,2,1,0:T(8,128)(2,1)S(1)}, bf16[1,1,16,32]{3,2,1,0:T(8,128)(2,1)S(1)}, u32[]{:S(2)}, u32[]{:S(2)}) collective-permute-start(bf16[1,1,16,32]{3,2,1,0:T(8,128)(2,1)S(1)} %get-tuple-element.115), channel_id=1, source_target_pairs={{0,8},{8,16},{16,24},{24,32},{32,40},{40,48},{48,56},{56,64},{64,7... | collective-permute-start | bytes 3080 | tf_op jit(solution)/shard_map/ppermute | solution.py:21
  233.2 8.8 %collective-permute-start.7 = (bf16[1,1,16,32]{3,2,1,0:T(8,128)(2,1)S(1)}, bf16[1,1,16,32]{3,2,1,0:T(8,128)(2,1)S(1)}, u32[]{:S(2)}, u32[]{:S(2)}) collective-permute-start(bf16[1,1,16,32]{3,2,1,0:T(8,128)(2,1)S(1)} %get-tuple-element.116), channel_id=1, source_target_pairs={{8,0},{16,8},{24,16},{32,24},{40,32},{48,40},{56,48},{64,56},{72,6... | collective-permute-start | bytes 3080 | tf_op jit(solution)/shard_map/ppermute | solution.py:24
  242.3 9.6 %collective-permute-start.8 = (bf16[1,1,8,16]{3,2,1,0:T(8,128)(2,1)S(1)}, bf16[1,1,8,16]{3,2,1,0:T(8,128)(2,1)S(1)}, u32[]{:S(2)}, u32[]{:S(2)}) collective-permute-start(bf16[1,1,8,16]{3,2,1,0:T(8,128)(2,1)S(1)} %get-tuple-element.126), channel_id=1, source_target_pairs={{0,8},{8,16},{16,24},{24,32},{32,40},{40,48},{48,56},{56,64},{64,7... | collective-permute-start | bytes 776 | tf_op jit(solution)/shard_map/ppermute | solution.py:21
  244.2 8.8 %collective-permute-start.9 = (bf16[1,1,8,16]{3,2,1,0:T(8,128)(2,1)S(1)}, bf16[1,1,8,16]{3,2,1,0:T(8,128)(2,1)S(1)}, u32[]{:S(2)}, u32[]{:S(2)}) collective-permute-start(bf16[1,1,8,16]{3,2,1,0:T(8,128)(2,1)S(1)} %get-tuple-element.126), channel_id=1, source_target_pairs={{8,0},{16,8},{24,16},{32,24},{40,32},{48,40},{56,48},{64,56},{72,6... | collective-permute-start | bytes 776 | tf_op jit(solution)/shard_map/ppermute | solution.py:24
  253.1 9.6 %collective-permute-start.10 = (bf16[1,1,8,16]{3,2,1,0:T(8,128)(2,1)S(1)}, bf16[1,1,8,16]{3,2,1,0:T(8,128)(2,1)S(1)}, u32[]{:S(2)}, u32[]{:S(2)}) collective-permute-start(bf16[1,1,8,16]{3,2,1,0:T(8,128)(2,1)S(1)} %get-tuple-element.16), channel_id=1, source_target_pairs={{0,8},{8,16},{16,24},{24,32},{32,40},{40,48},{48,56},{56,64},{64,7... | collective-permute-start | bytes 776 | tf_op jit(solution)/shard_map/ppermute | solution.py:21
  255.0 8.8 %collective-permute-start.11 = (bf16[1,1,8,16]{3,2,1,0:T(8,128)(2,1)S(1)}, bf16[1,1,8,16]{3,2,1,0:T(8,128)(2,1)S(1)}, u32[]{:S(2)}, u32[]{:S(2)}) collective-permute-start(bf16[1,1,8,16]{3,2,1,0:T(8,128)(2,1)S(1)} %get-tuple-element.16), channel_id=1, source_target_pairs={{8,0},{16,8},{24,16},{32,24},{40,32},{48,40},{56,48},{64,56},{72,6... | collective-permute-start | bytes 776 | tf_op jit(solution)/shard_map/ppermute | solution.py:24
  264.3 9.4 %collective-permute-start.12 = (bf16[1,1,16,32]{3,2,1,0:T(8,128)(2,1)S(1)}, bf16[1,1,16,32]{3,2,1,0:T(8,128)(2,1)S(1)}, u32[]{:S(2)}, u32[]{:S(2)}) collective-permute-start(bf16[1,1,16,32]{3,2,1,0:T(8,128)(2,1)S(1)} %get-tuple-element.113), channel_id=1, source_target_pairs={{0,8},{8,16},{16,24},{24,32},{32,40},{40,48},{48,56},{56,64},{64,7... | collective-permute-start | bytes 3080 | tf_op jit(solution)/shard_map/ppermute | solution.py:21
  266.2 8.8 %collective-permute-start.13 = (bf16[1,1,16,32]{3,2,1,0:T(8,128)(2,1)S(1)}, bf16[1,1,16,32]{3,2,1,0:T(8,128)(2,1)S(1)}, u32[]{:S(2)}, u32[]{:S(2)}) collective-permute-start(bf16[1,1,16,32]{3,2,1,0:T(8,128)(2,1)S(1)} %get-tuple-element.114), channel_id=1, source_target_pairs={{8,0},{16,8},{24,16},{32,24},{40,32},{48,40},{56,48},{64,56},{72,6... | collective-permute-start | bytes 3080 | tf_op jit(solution)/shard_map/ppermute | solution.py:24
  275.7 9.5 %collective-permute-start.14 = (bf16[1,1,32,64]{3,2,1,0:T(8,128)(2,1)S(1)}, bf16[1,1,32,64]{3,2,1,0:T(8,128)(2,1)S(1)}, u32[]{:S(2)}, u32[]{:S(2)}) collective-permute-start(bf16[1,1,32,64]{3,2,1,0:T(8,128)(2,1)S(1)} %get-tuple-element.88), channel_id=1, source_target_pairs={{0,8},{8,16},{16,24},{24,32},{32,40},{40,48},{48,56},{56,64},{64,7... | collective-permute-start | bytes 12296 | tf_op jit(solution)/shard_map/ppermute | solution.py:21
  277.6 8.9 %collective-permute-start.15 = (bf16[1,1,32,64]{3,2,1,0:T(8,128)(2,1)S(1)}, bf16[1,1,32,64]{3,2,1,0:T(8,128)(2,1)S(1)}, u32[]{:S(2)}, u32[]{:S(2)}) collective-permute-start(bf16[1,1,32,64]{3,2,1,0:T(8,128)(2,1)S(1)} %get-tuple-element.89), channel_id=1, source_target_pairs={{8,0},{16,8},{24,16},{32,24},{40,32},{48,40},{56,48},{64,56},{72,6... | collective-permute-start | bytes 12296 | tf_op jit(solution)/shard_map/ppermute | solution.py:24
  287.6 9.8 %collective-permute-start.16 = (bf16[1,1,64,128]{2,1,3,0:T(2,128)(2,1)S(1)}, bf16[1,1,64,128]{2,1,3,0:T(2,128)(2,1)S(1)}, u32[]{:S(2)}, u32[]{:S(2)}) collective-permute-start(bf16[1,1,64,128]{2,1,3,0:T(2,128)(2,1)S(1)} %get-tuple-element.56), channel_id=1, source_target_pairs={{0,8},{8,16},{16,24},{24,32},{32,40},{40,48},{48,56},{56,64},{64,7... | collective-permute-start | bytes 49160 | tf_op jit(solution)/shard_map/ppermute | solution.py:21
  289.5 9.4 %collective-permute-start.17 = (bf16[1,1,64,128]{2,1,3,0:T(2,128)(2,1)S(1)}, bf16[1,1,64,128]{2,1,3,0:T(2,128)(2,1)S(1)}, u32[]{:S(2)}, u32[]{:S(2)}) collective-permute-start(bf16[1,1,64,128]{2,1,3,0:T(2,128)(2,1)S(1)} %get-tuple-element.57), channel_id=1, source_target_pairs={{8,0},{16,8},{24,16},{32,24},{40,32},{48,40},{56,48},{64,56},{72,6... | collective-permute-start | bytes 49160 | tf_op jit(solution)/shard_map/ppermute | solution.py:24
  311.4 19.3 %all-to-all-start = ((bf16[8,2,32768]{2,1,0:T(2,128)(2,1)}), bf16[8,2,32768]{2,1,0:T(2,128)(2,1)S(1)}, u32[]{:S(2)}, u32[]{:S(2)}) async-start(bf16[8,2,32768]{2,1,0:T(2,128)(2,1)} %reshape.820), calls=%async_computation | async-start | bytes 2097152 | tf_op jit(solution)/shard_map/all_to_all | solution.py:102
  331.7 1.3 copy-start
